TPU v7x, 512 devices: a whole 4x4x16 slice. The times are simulated.
512 devices in a mesh: attn: 8 (over y, core), exp: 16 (over z), seq: 4 (over x).
Axes of the slice: x: 4, y: 4, z: 16, core: 2. Of those that a mesh axis runs over, the one named last changes fastest.
Arguments:
- tokens: bfloat16 [256, 6144], P(('attn', 'exp'), 'seq'), may hold values from -6 to 6
- modality: int32 [256], P(('attn', 'exp')), may hold values from 0 to 1, as said below
- cotangent: bfloat16 [256, 6144], P(('attn', 'exp'), 'seq'), may hold values from -6 to 6
- gate_speech: bfloat16 [6144, 24576], P('seq', ('attn', 'exp')), may hold values from -0.078125 to 0.078125
- up_speech: bfloat16 [6144, 24576], P('seq', ('attn', 'exp')), may hold values from -0.078125 to 0.078125
- down_speech: bfloat16 [24576, 6144], P(('attn', 'exp'), 'seq'), may hold values from -0.078125 to 0.078125
- gate_text: bfloat16 [6144, 16384], P('seq', ('attn', 'exp')), may hold values from -0.078125 to 0.078125
- up_text: bfloat16 [6144, 16384], P('seq', ('attn', 'exp')), may hold values from -0.078125 to 0.078125
- down_text: bfloat16 [16384, 6144], P(('attn', 'exp'), 'seq'), may hold values from -0.09375 to 0.09375
Outputs:
- mixed: bfloat16 [256, 6144], P(('attn', 'exp'), 'seq')
- token_grad: bfloat16 [256, 6144], P(('attn', 'exp'), 'seq')
- down_speech_grad: bfloat16 [24576, 6144], P(('attn', 'exp'), 'seq')
- down_text_grad: bfloat16 [16384, 6144], P(('attn', 'exp'), 'seq')
Inputs may be any that keep to these rules, and one draw needn't show every extreme that they name: Exactly 160 tokens of the window have modality 0 and the other 96 have modality 1, at places drawn from the seed.
All inputs are finite; a program needn't handle non-finite values.
Results may differ from a plain program's by a relative error of at most 0.005.
Values may be sent and summed in bfloat16 or wider, within the bound.
A program may use at most 64 MiB of HBM per device.

v0:
```python
import jax
import jax.numpy as jnp
from jax import lax
from jax.sharding import PartitionSpec as P


def contract_first(left, right):
    return lax.dot_general(
        left, right, (((0,), (0,)), ((), ())), preferred_element_type=jnp.float32
    )


def contract_last(left, right):
    return lax.dot_general(
        left, right, (((1,), (1,)), ((), ())), preferred_element_type=jnp.float32
    )


def shards(
    tokens, modality, cotangent, gate_speech, up_speech, down_speech, gate_text, up_text, down_text
):
    rows, grads, kinds = (
        lax.all_gather(tokens, ("attn", "exp"), axis=0, tiled=True),
        lax.all_gather(cotangent, ("attn", "exp"), axis=0, tiled=True),
        lax.all_gather(modality, ("attn", "exp"), axis=0, tiled=True),
    )
    speech = (kinds == 0)[:, None]
    features = lax.all_gather(rows, "seq", axis=1, tiled=True)
    full_gs, full_us, full_gt, full_ut = (
        lax.all_gather(gate_speech, "seq", axis=0, tiled=True),
        lax.all_gather(up_speech, "seq", axis=0, tiled=True),
        lax.all_gather(gate_text, "seq", axis=0, tiled=True),
        lax.all_gather(up_text, "seq", axis=0, tiled=True),
    )
    zero = jnp.zeros_like(grads)
    speech_grads = jnp.where(speech, grads, zero)
    text_grads = jnp.where(speech, zero, grads)
    terms = (
        jnp.dot(features, full_gs, preferred_element_type=jnp.float32),
        jnp.dot(features, full_us, preferred_element_type=jnp.float32),
        jnp.dot(features, full_gt, preferred_element_type=jnp.float32),
        jnp.dot(features, full_ut, preferred_element_type=jnp.float32),
    )
    gs, us, gt, ut = terms
    hs = (jax.nn.silu(gs) * us).astype(jnp.bfloat16)
    ht = (jax.nn.silu(gt) * ut).astype(jnp.bfloat16)
    speech_out = jnp.dot(hs, down_speech, preferred_element_type=jnp.float32)
    text_out = jnp.dot(ht, down_text, preferred_element_type=jnp.float32)
    partial_out = jnp.where(speech, speech_out, text_out)
    mixed = lax.psum_scatter(partial_out, ("attn", "exp"), scatter_dimension=0, tiled=True).astype(
        jnp.bfloat16
    )
    dhs, dht = lax.psum(
        (contract_last(speech_grads, down_speech), contract_last(text_grads, down_text)), "seq"
    )
    sig_s = jax.nn.sigmoid(gs)
    sig_t = jax.nn.sigmoid(gt)
    dgs = (dhs * us * sig_s * (1.0 + gs * (1.0 - sig_s))).astype(jnp.bfloat16)
    dus = (dhs * jax.nn.silu(gs)).astype(jnp.bfloat16)
    dgt = (dht * ut * sig_t * (1.0 + gt * (1.0 - sig_t))).astype(jnp.bfloat16)
    dut = (dht * jax.nn.silu(gt)).astype(jnp.bfloat16)
    speech_back = contract_last(dgs, gate_speech) + contract_last(dus, up_speech)
    text_back = contract_last(dgt, gate_text) + contract_last(dut, up_text)
    partial_grad = speech_back + text_back
    token_grad = lax.psum_scatter(
        partial_grad, ("attn", "exp"), scatter_dimension=0, tiled=True
    ).astype(jnp.bfloat16)
    down_speech_grad = contract_first(hs, speech_grads).astype(jnp.bfloat16)
    down_text_grad = contract_first(ht, text_grads).astype(jnp.bfloat16)
    return (mixed, token_grad, down_speech_grad, down_text_grad)


def solution(mesh):
    return jax.shard_map(
        shards,
        mesh=mesh,
        in_specs=(
            P(("attn", "exp"), "seq"),
            P(("attn", "exp")),
            P(("attn", "exp"), "seq"),
            P("seq", ("attn", "exp")),
            P("seq", ("attn", "exp")),
            P(("attn", "exp"), "seq"),
            P("seq", ("attn", "exp")),
            P("seq", ("attn", "exp")),
            P(("attn", "exp"), "seq"),
        ),
        out_specs=(
            P(("attn", "exp"), "seq"),
            P(("attn", "exp"), "seq"),
            P(("attn", "exp"), "seq"),
            P(("attn", "exp"), "seq"),
        ),
        check_vma=False,
    )
```

profile of v0, /device:TPU:2, one launch (start us, length us, event | category | flops | bytes accessed | tf_op | source)
XLA Modules:
  0.0 866.6 jit_solution(7845797920021915052)
XLA Ops:
  7.2 0.0 copy-start
  7.2 0.0 all-gather.10.cloned.1.call-start
  7.2 0.7 all-gather.10.cloned.1.call-update
  7.9 0.0 all-gather.8.cloned.1.call-start
  8.0 100.8 %all-gather = bf16[128,2,1536]{2,1,0:T(2,128)(2,1)S(1)} all-gather(bf16[1,2,1536]{2,1,0:T(2,128)(2,1)} %bitcast.24), channel_id=1, replica_groups=mesh['attn'=8,'exp'=16,'seq'=4] {'attn','exp'}, dimensions={0}, use_global_device_ids=true | all-gather | bytes 792576 | tf_op jit(solution)/shard_map/all_gather | solution.py:23
  108.8 1.2 reshape.13
  110.0 0.0 all-gather.8.cloned.1.call-update
  110.0 0.0 all-gather.12.cloned.1.call-start
  110.0 0.7 all-gather.12.cloned.1.call-update
  110.7 0.0 copy-start.15
  110.8 0.0 copy-start.16
  110.8 0.0 all-gather.14.cloned.1.call-start
  110.8 0.5 all-gather.14.cloned.1.call-update
  111.4 0.0 all-gather.16.cloned.1.call-start
  111.4 0.5 all-gather.16.cloned.1.call-update
  111.9 0.0 all-reduce.8.cloned.1.call-start
  112.0 92.1 %all-gather.1 = bf16[128,2,1536]{2,1,0:T(2,128)(2,1)S(1)} all-gather(bf16[1,2,1536]{2,1,0:T(2,128)(2,1)S(1)} %bitcast.25), channel_id=1, replica_groups=mesh['attn'=8,'exp'=16,'seq'=4] {'attn','exp'}, dimensions={0}, use_global_device_ids=true | all-gather | bytes 792576 | tf_op jit(solution)/shard_map/all_gather | solution.py:24
  204.1 0.3 reshape.15
  204.4 0.7 fusion.19
  205.8 0.2 dynamic-update-slice
  206.1 23.4 %all-reduce = s32[256]{0:T(256)S(1)} all-reduce(s32[256]{0:T(256)S(1)} %dynamic-update-slice), channel_id=1, replica_groups=mesh['attn'=8,'exp'=16,'seq'=4] {'attn','exp'}, use_global_device_ids=true, to_apply=%add | all-reduce | flops 256 | bytes 2048
  229.5 1.1 fusion.2
  230.6 1.2 fusion.1
  231.7 0.0 all-reduce.8.cloned.1.call-update
  232.4 0.0 all-gather.10.cloned.1.call-done
  232.4 0.0 all-gather.8.cloned.1.call-done
  232.5 3.8 fusion.20
  236.3 0.0 all-gather.12.cloned.1.call-done
  236.3 4.6 multiply_convert_fusion.2
  240.9 1.6 fusion.21
  242.4 3.3 fusion.22
  245.8 20.4 %all-gather.16.cloned.1.call-done = bf16[6144,128]{1,0:T(8,128)(2,1)} async-done(((bf16[1536,128]{1,0:T(8,128)(2,1)}), bf16[6144,128]{1,0:T(8,128)(2,1)}) %all-gather.16.cloned.1.call-update) | async-done | bytes 1572880 | tf_op jit(solution)/shard_map/all_gather | solution.py:33
  266.2 4.1 multiply_convert_fusion.5
  270.3 0.4 convolution_select_fusion
  270.6 0.8 copy-done.10
  271.4 1.1 convolution_convert_fusion.1
  272.5 1.2 convolution_convert_fusion
  273.7 52.4 %all-reduce.8.cloned.1.call-done = (f32[256,192]{0,1:T(8,128)}, f32[256,128]{1,0:T(8,128)}) async-done(((f32[256,192]{0,1:T(8,128)}, f32[256,128]{1,0:T(8,128)}), (f32[256,192]{0,1:T(8,128)}, f32[256,128]{1,0:T(8,128)})) %all-reduce.8.cloned.1.call-update) | async-done | bytes 327696 | tf_op jit(solution)/shard_map/psum | solution.py:53
  326.1 1.6 fusion.5
  327.8 0.4 convolution_add_fusion.1
  328.2 0.5 copy-done.6
  328.7 0.0 copy-done.11
  328.8 0.1 copy-done.12
  328.8 0.4 fusion.7
  329.2 0.0 copy-done.7
  329.3 1.6 fusion
  330.8 527.6 %all-reduce.9 = (bf16[256,1536]{1,0:T(8,128)(2,1)S(1)}, bf16[256,1536]{1,0:T(8,128)(2,1)}) all-reduce(f32[256,1536]{1,0:T(8,128)S(1)} %convolution_select_fusion, f32[256,1536]{1,0:T(8,128)} %fusion), channel_id=2, replica_groups=mesh['attn'=8,'exp'=16,'seq'=4] {'attn','exp'}, use_global_device_ids=true, to_apply=%region_0.1.clone | all-reduce | flops 786432 | bytes 4718592
  858.4 1.3 dynamic-slice_convert_fusion
  (29 shorter events, 0.1 us)
Async XLA Ops:
  7.2 223.4 %copy-start = (bf16[192,1536]{1,0:T(8,128)(2,1)S(1)}, bf16[192,1536]{1,0:T(8,128)(2,1)}, u32[]{:S(2)}) copy-start(bf16[192,1536]{1,0:T(8,128)(2,1)} %param.14) | copy-start | bytes 1769476
  7.2 225.3 %all-gather.10.cloned.1.call-start = ((), (), s32[]{:S(2)}) async-start(), calls=%async_computation.1 | async-start | bytes 2949120 | tf_op jit(solution)/shard_map/all_gather | solution.py:30
  7.9 224.5 %all-gather.8.cloned.1.call-start = ((), (), s32[]{:S(2)}) async-start(), calls=%async_computation | async-start | bytes 3932160 | tf_op jit(solution)/shard_map/all_gather | solution.py:28
  108.8 3.2 copy-start.14
  110.0 126.3 %all-gather.12.cloned.1.call-start = ((), (), s32[]{:S(2)}) async-start(), calls=%async_computation.2 | async-start | bytes 2949120 | tf_op jit(solution)/shard_map/all_gather | solution.py:31
  110.7 93.7 %copy-start.15 = (u32[512]{0:T(512)S(1)}, u32[512]{0:T(512)}, u32[]{:S(2)}) copy-start(u32[512]{0:T(512)} %constant.21) | copy-start | bytes 6148
  110.8 95.1 %copy-start.16 = (s32[2]{0:T(128)S(1)}, s32[2]{0:T(128)}, u32[]{:S(2)}) copy-start(s32[2]{0:T(128)} %param.10) | copy-start | bytes 28
  110.8 118.7 %copy-start.13 = (bf16[128,1536]{1,0:T(8,128)(2,1)S(1)}, bf16[128,1536]{1,0:T(8,128)(2,1)}, u32[]{:S(2)}) copy-start(bf16[128,1536]{1,0:T(8,128)(2,1)} %param.17) | copy-start | bytes 1179652
  110.8 131.7 %all-gather.14.cloned.1.call-start = ((), (), s32[]{:S(2)}) async-start(), calls=%async_computation.3 | async-start | bytes 1966080 | tf_op jit(solution)/shard_map/all_gather | solution.py:32
  111.4 154.8 %all-gather.16.cloned.1.call-start = ((), (), s32[]{:S(2)}) async-start(), calls=%async_computation.4 | async-start | bytes 1966080 | tf_op jit(solution)/shard_map/all_gather | solution.py:33
  111.9 214.2 %all-reduce.8.cloned.1.call-start = ((), (), s32[]{:S(2)}) async-start(), calls=%async_computation.5 | async-start | bytes 655360 | tf_op jit(solution)/shard_map/psum | solution.py:53
  204.4 27.3 %copy-start.9 = (bf16[256,1536]{1,0:T(8,128)(2,1)}, bf16[256,1536]{1,0:T(8,128)(2,1)S(1)}, u32[]{:S(2)}) copy-start(bf16[256,1536]{1,0:T(8,128)(2,1)S(1)} %reshape.15) | copy-start | bytes 2359300
  236.3 4.6 copy-start.4
  266.2 4.1 copy-start.1
  270.3 1.1 copy-start.10
  271.4 54.7 %copy-start.2 = (bf16[1536,192]{0,1:T(8,128)(2,1)S(1)}, bf16[1536,192]{0,1:T(8,128)(2,1)}, u32[]{:S(2)}) copy-start(bf16[1536,192]{0,1:T(8,128)(2,1)} %param.12) | copy-start | bytes 1769476
  273.7 54.0 %copy-start.3 = (bf16[1536,192]{0,1:T(8,128)(2,1)S(1)}, bf16[1536,192]{0,1:T(8,128)(2,1)}, u32[]{:S(2)}) copy-start(bf16[1536,192]{0,1:T(8,128)(2,1)} %param.13) | copy-start | bytes 1769476
  326.1 1.6 copy-start.5
  326.1 1.6 copy-start.8
  327.7 1.0 copy-start.6
  327.8 1.0 copy-start.11
  327.8 1.1 copy-start.12
  328.2 1.1 copy-start.7
Sparse Core Ops, SparseCore 0:
  10.1 44.2 all-gather.9
  110.1 40.5 all-gather.7
  152.8 40.8 all-gather.11
  195.6 34.1 all-gather.13
  231.8 34.3 all-gather.15
  268.4 57.6 all-reduce.7
where the time goes:
time: 867 us
  blocking collectives  744 us (86%)
  waiting for transfers between devices  75.3 us (9%)
  matrix products  26.2 us (3%)
  between operations  15.7 us (2%)
    unnamed x2, blocking collectives  551 us
    all_gather x1, blocking collectives, shards(): lax.all_gather(tokens, ('attn', 'exp'), axis=0, tiled=True)  101 us
    all_gather x1, blocking collectives, shards(): lax.all_gather(cotangent, ('attn', 'exp'), axis=0, tiled=True)  92.1 us
    psum x1, waiting for transfers between devices, shards(): lax.psum((contract_last(speech_grads, down_speech), contract_last(text_gr...  52.4 us
    all_gather x1, waiting for transfers between devices, shards(): lax.all_gather(up_text, 'seq', axis=0, tiled=True)  20.4 us
  transfers between devices with their start and end apart: 6, of which 2 were waited for; matrix products, arithmetic and copies ran while one was open for 3% of the time, Pallas kernels for 0%

commit v1 on v0

v1 whole, which is shorter than its diff:
```python
import functools

import jax
import jax.numpy as jnp
from jax import lax
from jax.experimental import pallas as pl
from jax.experimental.pallas import tpu as pltpu
from jax.sharding import PartitionSpec as P

BF = jnp.bfloat16
F32 = jnp.float32
MESH = pl.DeviceIdType.MESH
LANE = 128
TOK, COT, OUT, GRAD = range(4)


def nn(left, right):
    return lax.dot_general(left, right, (((1,), (0,)), ((), ())), preferred_element_type=F32)


def nt(left, right):
    return lax.dot_general(left, right, (((1,), (1,)), ((), ())), preferred_element_type=F32)


def tn(left, right):
    return lax.dot_general(left, right, (((0,), (0,)), ((), ())), preferred_element_type=F32)


def remote(src, dst, send, recv, device):
    return pltpu.make_async_remote_copy(
        src_ref=src, dst_ref=dst, send_sem=send, recv_sem=recv, device_id=device, device_id_type=MESH
    )


def kernel(
    NY, E, S,
    tok, mod, cot, w_gs, w_us, w_ds, w_gt, w_ut, w_dt,
    mixed_o, grad_o, dsg_o, dtg_o,
    gs, us, gt, ut, down,
    tok_blk, cot_blk, tok_z, cot_z, flat, xt, ct,
    p1, p2, r1, r2, gu, hb, gb,
    sib_src, sib_dst, acc, y_src, y_dst, z_src, z_dst, hcat,
    wsem, zsem, ysem, csem, xsem,
):
    attn, z, x = lax.axis_index("attn"), lax.axis_index("exp"), lax.axis_index("seq")
    y, c = attn // 2, attn % 2
    other = 1 - c
    R, D = cot_blk.shape
    RB = E * R
    HALF = NY * RB
    CH = 2 * HALF // S
    FS, FT = gs.shape[0], gt.shape[1]
    FX = FS - FT
    NC = 256 if D % 256 == 0 else D

    local = [
        pltpu.make_async_copy(tok, tok_blk.at[:, pl.ds(0, D)], wsem.at[0]),
        pltpu.make_async_copy(cot, cot_blk, wsem.at[1]),
        pltpu.make_async_copy(w_gs, gs, wsem.at[2]),
        pltpu.make_async_copy(w_us, us, wsem.at[3]),
        pltpu.make_async_copy(w_gt, gt, wsem.at[4]),
        pltpu.make_async_copy(w_ut, ut, wsem.at[5]),
        pltpu.make_async_copy(w_ds.at[pl.ds(0, FT)], down.at[pl.ds(0, FT)], wsem.at[6]),
        pltpu.make_async_copy(w_dt, down.at[pl.ds(FT, FT)], wsem.at[7]),
        pltpu.make_async_copy(w_ds.at[pl.ds(FT, FX)], down.at[pl.ds(2 * FT, FX)], wsem.at[8]),
    ]
    for copy in local:
        copy.start()

    def greet(axis, count, me, scale, base):
        def body(d, _):
            peer = lax.rem(me + d, count)
            pl.semaphore_signal(
                barrier, inc=1, device_id={axis: peer * scale + base}, device_id_type=MESH
            )
            return 0

        lax.fori_loop(1, count, body, 0)

    barrier = pltpu.get_barrier_semaphore()
    greet("exp", E, z, 1, 0)
    greet("attn", NY, y, 2, c)
    greet("seq", S, x, 1, 0)
    pl.semaphore_signal(barrier, inc=1, device_id={"attn": y * 2 + other}, device_id_type=MESH)

    local[0].wait()
    kind = jnp.concatenate(
        [jnp.full((1, LANE), mod[i].astype(F32), F32) for i in range(R)], axis=0
    )
    tok_blk[:, D:] = kind.astype(BF)
    local[1].wait()
    pl.semaphore_wait(barrier, (E - 1) + (NY - 1) + (S - 1) + 1)

    def z_send(k, src, dst):
        def body(d, _):
            t = lax.rem(z + d, E)
            remote(src(t), dst.at[z], zsem.at[k, 0, t], zsem.at[k, 1, z], {"exp": t}).start()
            return 0

        lax.fori_loop(1, E, body, 0)

    def z_each(k, src, dst, recv):
        def body(d, _):
            t = lax.rem(z + d, E)
            copy = remote(src(t), dst.at[t], zsem.at[k, 0, t], zsem.at[k, 1, t], {"exp": t})
            copy.wait_recv() if recv else copy.wait_send()
            return 0

        lax.fori_loop(1, E, body, 0)

    def y_copy(k, t, src, dst, mark):
        return remote(src, dst, ysem.at[k, 0, t], ysem.at[k, 1, mark], {"attn": t * 2 + c})

    def c_copy(k, i, src, dst):
        return remote(src, dst, csem.at[k, 0, i], csem.at[k, 1, i], {"attn": y * 2 + other})

    def x_copy(k, t, src, dst, mark):
        return remote(src, dst, xsem.at[k, 0, t], xsem.at[k, 1, mark], {"seq": t})

    def ys():
        return [lax.rem(y + d, NY) for d in range(1, NY)]

    def xs():
        return [lax.rem(x + d, S) for d in range(1, S)]

    def block(ref, core, yy):
        return ref.at[pl.ds(pl.multiple_of(core * HALF + yy * RB, RB), RB)]

    def rows(ref, i):
        return ref.at[pl.ds(pl.multiple_of(i * CH, CH), CH)]

    z_send(TOK, lambda t: tok_blk, tok_z)
    z_send(COT, lambda t: cot_blk, cot_z)
    tok_z[z] = tok_blk[...]
    cot_z[z] = cot_blk[...]

    def assemble(k, blk, buf, whole):
        z_each(k, lambda t: blk, buf, True)
        width = blk.shape[1]
        for i in range(E):
            flat[i * R : (i + 1) * R, :width] = buf[i].astype(F32)
        mine = block(whole, c, y)
        mine[...] = flat[:, :width].astype(BF)
        for t in ys():
            y_copy(k, t, mine, mine, y).start()
        c_copy(k, y, mine, mine).start()

    assemble(TOK, tok_blk, tok_z, xt)
    assemble(COT, cot_blk, cot_z, ct)

    def pass_on(k, whole):
        for t in ys():
            got = block(whole, c, t)
            y_copy(k, t, got, got, t).wait_recv()
            c_copy(k, t, got, got).start()

    def from_sibling(k, whole):
        for t in range(NY):
            got = block(whole, other, t)
            c_copy(k, t, got, got).wait_recv()

    def half_rows(core):
        return pl.ds(pl.multiple_of(core * HALF, HALF), HALF)

    def project(core):
        r = half_rows(core)
        feats = xt[r, :D]
        speech = xt[r, D:].astype(F32) < 0.5
        a, b = nt(feats, gs[...]), nt(feats, us[...])
        p1[r, 0:FT] = jnp.where(speech, a[:, :FT], nn(feats, gt[...]))
        p1[r, FT : 2 * FT] = jnp.where(speech, b[:, :FT], nn(feats, ut[...]))
        p1[r, 2 * FT :] = jnp.concatenate([a[:, FT:], b[:, FT:]], axis=1)

    def hidden_grad(core):
        r = half_rows(core)
        speech = xt[r, D:].astype(F32) < 0.5
        d = nt(ct[r, :], down[...])
        p2[r, 0:FT] = jnp.where(speech, d[:, :FT], d[:, FT : 2 * FT])
        tail = d[:, 2 * FT :]
        p2[r, FT:] = jnp.concatenate([tail, jnp.zeros_like(tail)], axis=1)

    for copy in local[2:6]:
        copy.wait()
    pass_on(TOK, xt)
    project(c)
    from_sibling(TOK, xt)
    project(other)
    for t in xs():
        x_copy(0, t, rows(p1, t), r1.at[x], x).start()

    for copy in local[6:]:
        copy.wait()
    pass_on(COT, ct)
    hidden_grad(c)
    from_sibling(COT, ct)
    hidden_grad(other)
    for t in xs():
        x_copy(1, t, rows(p2, t), r2.at[x], x).start()

    def split(v):
        return v[:, :FX], v[:, FX : 2 * FX]

    total = rows(p1, x)[...]
    for t in xs():
        x_copy(0, t, r1.at[t], r1.at[t], t).wait_recv()
        total += r1[t]
    gu[...] = total
    g, u = total[:, :FT], total[:, FT : 2 * FT]
    ge, ue = split(total[:, 2 * FT :])
    he = jax.nn.silu(ge) * ue
    mine = rows(hb, x)
    mine[:, 0:FT] = (jax.nn.silu(g) * u).astype(BF)
    mine[:, FT:] = jnp.concatenate([he, jnp.zeros_like(he)], axis=1).astype(BF)
    for t in xs():
        x_copy(2, t, mine, mine, x).start()

    total = rows(p2, x)[...]
    for t in xs():
        x_copy(1, t, r2.at[t], r2.at[t], t).wait_recv()
        total += r2[t]

    def back(dh, g, u):
        sig = jax.nn.sigmoid(g)
        return dh * u * sig * (1.0 + g * (1.0 - sig)), dh * (g * sig)

    dg, du = back(total[:, :FT], gu[:, :FT], gu[:, FT : 2 * FT])
    ge, ue = split(gu[:, 2 * FT :])
    dge, due = back(total[:, FT : FT + FX], ge, ue)
    mine_g = rows(gb, x)
    mine_g[:, 0:FT] = dg.astype(BF)
    mine_g[:, FT : 2 * FT] = du.astype(BF)
    mine_g[:, 2 * FT :] = jnp.concatenate([dge, due], axis=1).astype(BF)
    for t in xs():
        x_copy(3, t, mine_g, mine_g, x).start()

    def columns(n):
        return pl.ds(pl.multiple_of(n * NC, NC), NC)

    def out_half(core, store):
        r = half_rows(core)
        text = xt[r, D:]
        speech = (1.0 - text.astype(F32)).astype(BF)
        h = hb[r, 0:FT]
        hcat[r, 0:FT] = h * speech
        hcat[r, FT : 2 * FT] = h * text
        hcat[r, 2 * FT :] = hb[r, FT : FT + FX] * speech[:, :FX]
        left = hcat[r, :]

        def body(n, _):
            store(n, nn(left, down[:, columns(n)]))
            return 0

        lax.fori_loop(0, D // NC, body, 0)

    def grad_half(core, store):
        r = half_rows(core)
        text = xt[r, D:]
        speech = (1.0 - text.astype(F32)).astype(BF)
        dg, du = gb[r, 0:FT], gb[r, FT : 2 * FT]
        dge, due = split(gb[r, 2 * FT :])
        dgs = jnp.concatenate([dg * speech, dge * speech[:, :FX]], axis=1)
        dus = jnp.concatenate([du * speech, due * speech[:, :FX]], axis=1)
        dgt, dut = dg * text, du * text

        def body(n, _):
            w = columns(n)
            store(
                n,
                nn(dgs, gs[:, w]) + nn(dus, us[:, w]) + nt(dgt, gt[w, :]) + nt(dut, ut[w, :]),
            )
            return 0

        lax.fori_loop(0, D // NC, body, 0)

    def partials(k, half):
        def to_sibling(n, v):
            sib_src[k, :, columns(n)] = v.astype(BF)

        def keep(n, v):
            acc[k, :, columns(n)] = v

        half(other, to_sibling)
        c_copy(2 + k, 0, sib_src.at[k], sib_dst.at[k]).start()
        half(c, keep)

    def over_y(k):
        c_copy(2 + k, 0, sib_src.at[k], sib_dst.at[k]).wait_recv()

        def body(n, _):
            w = columns(n)
            v = acc[k, :, w] + sib_dst[k, :, w].astype(F32)
            acc[k, :, w] = v
            y_src[k, :, w] = v.astype(BF)
            return 0

        lax.fori_loop(0, D // NC, body, 0)
        for t in ys():
            y_copy(2 + k, t, y_part(y_src, k, t), y_dst.at[k, y], y).start()

    def y_part(ref, k, t):
        return ref.at[k, pl.ds(pl.multiple_of(t * RB, RB), RB)]

    def over_z(k):
        total = y_part(acc, k, y)[...]
        for t in ys():
            y_copy(2 + k, t, y_dst.at[k, t], y_dst.at[k, t], t).wait_recv()
            total += y_dst[k, t].astype(F32)
        for i in range(E):
            z_src[k, i] = total[i * R : (i + 1) * R].astype(BF)
        z_send(2 + k, lambda t: z_src.at[k, t], z_dst.at[k])
        z_dst[k, z] = z_src[k, z]

    def finish(k, out):
        z_each(2 + k, lambda t: z_src.at[k, t], z_dst.at[k], True)
        total = z_dst[k, 0].astype(F32)
        for i in range(1, E):
            total += z_dst[k, i].astype(F32)
        out[...] = total.astype(BF)

    for t in xs():
        got = rows(hb, t)
        x_copy(2, t, got, got, t).wait_recv()
    partials(0, out_half)
    for t in xs():
        got = rows(gb, t)
        x_copy(3, t, got, got, t).wait_recv()
    over_y(0)
    partials(1, grad_half)
    over_y(1)

    def down_grad(n, _):
        w = columns(n)
        v = tn(hcat[...], ct[:, w]).astype(BF)
        dsg_o[0:FT, w] = v[0:FT]
        dtg_o[:, w] = v[FT : 2 * FT]
        dsg_o[FT:, w] = v[2 * FT :]
        return 0

    lax.fori_loop(0, D // NC, down_grad, 0)

    over_z(0)
    over_z(1)
    finish(0, mixed_o)
    finish(1, grad_o)

    z_each(TOK, lambda t: tok_blk, tok_z, False)
    z_each(COT, lambda t: cot_blk, cot_z, False)
    for k in range(2):
        z_each(2 + k, lambda t: z_src.at[k, t], z_dst.at[k], False)
    mine = block(xt, c, y)
    mine_c = block(ct, c, y)
    for t in ys():
        y_copy(TOK, t, mine, mine, t).wait_send()
        y_copy(COT, t, mine_c, mine_c, t).wait_send()
        for k in range(2):
            y_copy(2 + k, t, y_part(y_src, k, t), y_dst.at[k, t], t).wait_send()
    for t in range(NY):
        got, got_c = block(xt, c, t), block(ct, c, t)
        c_copy(TOK, t, got, got).wait_send()
        c_copy(COT, t, got_c, got_c).wait_send()
    for k in range(2):
        c_copy(2 + k, 0, sib_src.at[k], sib_dst.at[k]).wait_send()
    for t in xs():
        x_copy(0, t, rows(p1, t), r1.at[t], t).wait_send()
        x_copy(1, t, rows(p2, t), r2.at[t], t).wait_send()
        got, got_g = rows(hb, x), rows(gb, x)
        x_copy(2, t, got, got, t).wait_send()
        x_copy(3, t, got_g, got_g, t).wait_send()


def shards(NY, E, S, tokens, modality, cotangent, *weights):
    R, D = tokens.shape
    gs, us, ds, gt, ut, dt = weights
    gs, us = gs.T, us.T
    FS, FT = gs.shape[0], gt.shape[1]
    RB = E * R
    HALF = NY * RB
    T = 2 * HALF
    CH = T // S
    DMA = pltpu.SemaphoreType.DMA
    hbm_spec = pl.BlockSpec(memory_space=pltpu.HBM)
    vmem_spec = pl.BlockSpec(memory_space=pltpu.VMEM)
    return pl.pallas_call(
        functools.partial(kernel, NY, E, S),
        out_shape=(
            jax.ShapeDtypeStruct((R, D), BF),
            jax.ShapeDtypeStruct((R, D), BF),
            jax.ShapeDtypeStruct(ds.shape, BF),
            jax.ShapeDtypeStruct(dt.shape, BF),
        ),
        in_specs=[hbm_spec, pl.BlockSpec(memory_space=pltpu.SMEM)] + [hbm_spec] * 7,
        out_specs=[vmem_spec] * 4,
        scratch_shapes=[
            pltpu.VMEM(gs.shape, BF),
            pltpu.VMEM(us.shape, BF),
            pltpu.VMEM(gt.shape, BF),
            pltpu.VMEM(ut.shape, BF),
            pltpu.VMEM((FS + FT, D), BF),
            pltpu.VMEM((R, D + LANE), BF),
            pltpu.VMEM((R, D), BF),
            pltpu.VMEM((E, R, D + LANE), BF),
            pltpu.VMEM((E, R, D), BF),
            pltpu.VMEM((RB, D + LANE), F32),
            pltpu.VMEM((T, D + LANE), BF),
            pltpu.VMEM((T, D), BF),
            pltpu.VMEM((T, 3 * FT), F32),
            pltpu.VMEM((T, 2 * FT), F32),
            pltpu.VMEM((S, CH, 3 * FT), F32),
            pltpu.VMEM((S, CH, 2 * FT), F32),
            pltpu.VMEM((CH, 3 * FT), F32),
            pltpu.VMEM((T, 2 * FT), BF),
            pltpu.VMEM((T, 3 * FT), BF),
            pltpu.VMEM((2, HALF, D), BF),
            pltpu.VMEM((2, HALF, D), BF),
            pltpu.VMEM((2, HALF, D), F32),
            pltpu.VMEM((2, HALF, D), BF),
            pltpu.VMEM((2, NY, RB, D), BF),
            pltpu.VMEM((2, E, R, D), BF),
            pltpu.VMEM((2, E, R, D), BF),
            pltpu.VMEM((T, FS + FT), BF),
            DMA((9,)),
            DMA((4, 2, E)),
            DMA((4, 2, NY)),
            DMA((4, 2, NY)),
            DMA((4, 2, S)),
        ],
        compiler_params=pltpu.CompilerParams(
            collective_id=0, has_side_effects=True, vmem_limit_bytes=62 << 20
        ),
    )(tokens, modality, cotangent, gs, us, ds, gt, ut, dt)


def solution(mesh):
    NY, E, S = mesh.shape["attn"] // 2, mesh.shape["exp"], mesh.shape["seq"]
    row = P(("attn", "exp"), "seq")
    col = P("seq", ("attn", "exp"))
    return jax.shard_map(
        functools.partial(shards, NY, E, S),
        mesh=mesh,
        in_specs=(row, P(("attn", "exp")), row, col, col, row, col, col, row),
        out_specs=(row, row, row, row),
        check_vma=False,
    )
```

time: 867 us -> 81.6 us (0.09)
  the two profiles are of different devices: /device:TPU:2 before, /device:TPU:1 now
where the time goes in v1:
time: 81.6 us; the launch traced here: 81.2 us
  Pallas kernels  75.9 us (93%)
  local copies, waits for them, and re-layouts  4.69 us (6%)
    pallas_call x1, Pallas kernels, shards(): pl.pallas_call(functools.partial(kernel, NY, E, S), out_shape=(jax.ShapeD...  75.9 us
    unnamed x10, local copies, waits for them, and re-layouts  4.69 us

profile of v1, /device:TPU:1, one launch (start us, length us, event | category | flops | bytes accessed | tf_op | source)
XLA Modules:
  0.0 81.2 jit_solution(588087671483323005)
XLA Ops:
  0.6 75.9 %shard_map.120 = (bf16[2,1536]{1,0:T(2,128)(2,1)}, bf16[2,1536]{1,0:T(2,128)(2,1)}, bf16[192,1536]{1,0:T(8,128)(2,1)}, bf16[128,1536]{1,0:T(8,128)(2,1)}) custom-call(bf16[2,1536]{1,0:T(2,128)(2,1)} %tok.1, s32[2]{0:T(128)} %mod.1, bf16[2,1536]{1,0:T(2,128)(2,1)} %cot.1, bf16[192,1536]{1,0:T(8,128)(2,1)} %bitcast.2, bf16[192,1536]{1,0:T(8,128)(2,1)} %bitcast.3, ...), custom_call_target="tpu_custom_call" | custom-call | tf_op jit(solution)/shard_map/pallas_call | solution.py:383
  76.5 0.0 copy-start.2
  76.5 0.7 copy-done.2
  77.2 0.0 copy-start.1
  77.2 0.6 copy.17
  77.8 0.1 copy-done.1
  77.9 0.6 copy.18
  78.5 0.0 copy-start
  78.5 2.0 %copy.19 = bf16[192,1536]{1,0:T(8,128)(2,1)} copy(bf16[192,1536]{1,0:T(8,128)(2,1)} %get-tuple-element.10) | data formatting | bytes 1179648
  80.5 0.0 copy-done
  80.5 0.7 copy.20
Async XLA Ops:
  76.5 0.7 copy-start.2
  77.2 0.7 copy-start.1
  78.5 2.0 %copy-start = (bf16[128,1536]{1,0:T(8,128)(2,1)S(1)}, bf16[128,1536]{1,0:T(8,128)(2,1)}, u32[]{:S(2)}) copy-start(bf16[128,1536]{1,0:T(8,128)(2,1)} %get-tuple-element.11) | copy-start | bytes 1179652

commit v2 on v1

v2 whole, which is shorter than its diff:
```python
import functools

import jax
import jax.numpy as jnp
from jax import lax
from jax.experimental import pallas as pl
from jax.experimental.pallas import tpu as pltpu
from jax.sharding import PartitionSpec as P

BF = jnp.bfloat16
F32 = jnp.float32
MESH = pl.DeviceIdType.MESH
LANE = 128
TOK, COT = range(2)


def nn(left, right):
    return lax.dot_general(left, right, (((1,), (0,)), ((), ())), preferred_element_type=F32)


def nt(left, right):
    return lax.dot_general(left, right, (((1,), (1,)), ((), ())), preferred_element_type=F32)


def far_first(count):
    return sorted(range(1, count), key=lambda d: -min(d, count - d))


def remote(src, dst, send, recv, device):
    return pltpu.make_async_remote_copy(
        src_ref=src, dst_ref=dst, send_sem=send, recv_sem=recv, device_id=device, device_id_type=MESH
    )


def kernel(
    NY, E, S,
    tok, mod, cot, w_gs, w_us, w_ds, w_gt, w_ut, w_dt,
    mixed_o, grad_o, dsg_o, dtg_o,
    gt, ut, wide, down,
    tok_blk, cot_blk, tok_z, cot_z, flat, xt, ct,
    p1, p2, p2b, r1, r2, gu, hb, gb,
    sib_src, sib_dst, acc, y_src, y_dst, z_src, z_dst, hcat, mixed, grad, dsg, dtg,
    wsem, osem, zsem, ysem, gsem, csem, xsem,
):
    attn, z, x = lax.axis_index("attn"), lax.axis_index("exp"), lax.axis_index("seq")
    y, c = attn // 2, attn % 2
    other = 1 - c
    R, D = cot_blk.shape
    RB = E * R
    RG = RB // 2
    HALF = NY * RB
    CH = 2 * HALF // S
    FS, FT = w_gs.shape[0], gt.shape[1]
    FX = FS - FT
    NC = 512 if D % 512 == 0 else D

    def load(src, at, size, dst, to, n):
        return pltpu.make_async_copy(src.at[pl.ds(at, size)], dst.at[pl.ds(to, size)], wsem.at[n])

    local = [
        pltpu.make_async_copy(tok, tok_blk.at[:, pl.ds(0, D)], wsem.at[0]),
        pltpu.make_async_copy(cot, cot_blk, wsem.at[1]),
        pltpu.make_async_copy(w_gt, gt, wsem.at[2]),
        pltpu.make_async_copy(w_ut, ut, wsem.at[3]),
        load(w_gs, 0, FT, wide, 0, 4),
        load(w_us, 0, FT, wide, FT, 5),
        load(w_gs, FT, FX, wide, 4 * FT, 6),
        load(w_us, FT, FX, wide, 4 * FT + FX, 7),
        load(w_ds, 0, FT, down, 0, 8),
        load(w_dt, 0, FT, down, FT, 9),
        load(w_ds, FT, FX, down, 2 * FT, 10),
    ]
    for copy in local:
        copy.start()
    stores = [
        pltpu.make_async_copy(dsg, dsg_o, osem.at[0]),
        pltpu.make_async_copy(dtg, dtg_o, osem.at[1]),
        pltpu.make_async_copy(mixed, mixed_o, osem.at[2]),
        pltpu.make_async_copy(grad, grad_o, osem.at[3]),
    ]

    def greet(axis, count, me, scale, base):
        def body(d, _):
            peer = lax.rem(me + d, count)
            pl.semaphore_signal(
                barrier, inc=1, device_id={axis: peer * scale + base}, device_id_type=MESH
            )
            return 0

        lax.fori_loop(1, count, body, 0)

    barrier = pltpu.get_barrier_semaphore()
    greet("exp", E, z, 1, 0)
    greet("attn", NY, y, 2, c)
    greet("seq", S, x, 1, 0)
    pl.semaphore_signal(barrier, inc=1, device_id={"attn": y * 2 + other}, device_id_type=MESH)

    local[0].wait()
    kind = jnp.concatenate(
        [jnp.full((1, LANE), mod[i].astype(F32), F32) for i in range(R)], axis=0
    )
    tok_blk[:, D:] = kind.astype(BF)
    local[1].wait()
    pl.semaphore_wait(barrier, (E - 1) + (NY - 1) + (S - 1) + 1)

    def ahead(s):
        return lax.rem(z + E + (s + 1) // 2 * (2 * (s % 2) - 1), E)

    def mirror(s):
        return jnp.where(s == E - 1, s, s + 2 * (s % 2) - 1)

    pending = []

    def drain():
        for wait in pending:
            wait()

    def go(copy):
        copy.start()
        pending.append(copy.wait_send)

    def z_copy(k, s, src, dst, to):
        return remote(src(s), dst.at[to], zsem.at[k, 0, s], zsem.at[k, 1, to], {"exp": ahead(s)})

    def z_send(k, src, dst, low, high):
        def start(i, _):
            s = high - 1 - i
            z_copy(k, s, src, dst, mirror(s)).start()
            return 0

        def wait(s, _):
            z_copy(k, s, src, dst, s).wait_send()
            return 0

        lax.fori_loop(0, high - low, start, 0)
        pending.append(lambda: lax.fori_loop(low, high, wait, 0))

    def z_wait(k, src, dst, low, high):
        def wait(s, _):
            z_copy(k, s, src, dst, s).wait_recv()
            return 0

        lax.fori_loop(low, high, wait, 0)

    def y_copy(k, group, t, src, dst, mark):
        return remote(
            src, dst, ysem.at[k, group, 0, t], ysem.at[k, group, 1, mark], {"attn": t * 2 + c}
        )

    def g_copy(k, group, i, ref):
        return remote(
            ref, ref, gsem.at[k, group, 0, i], gsem.at[k, group, 1, i], {"attn": y * 2 + other}
        )

    def c_copy(k, n):
        w = pl.ds(n * NC, NC)
        return remote(
            sib_src.at[k, :, w], sib_dst.at[k, :, w], csem.at[k, 0, n], csem.at[k, 1, n],
            {"attn": y * 2 + other},
        )

    def x_copy(k, t, src, dst, mark):
        return remote(src, dst, xsem.at[k, 0, t], xsem.at[k, 1, mark], {"seq": t})

    def ys():
        return [lax.rem(y + d, NY) for d in far_first(NY)]

    def xs():
        return [lax.rem(x + d, S) for d in far_first(S)]

    def block(ref, core, yy, group):
        return ref.at[pl.ds(pl.multiple_of(core * HALF + yy * RB + group * RG, RG), RG)]

    def rows(ref, i):
        return ref.at[pl.ds(pl.multiple_of(i * CH, CH), CH)]

    z_send(TOK, lambda s: tok_blk, tok_z, 1, E)
    z_send(COT, lambda s: cot_blk, cot_z, 1, E)
    tok_z[0] = tok_blk[...]
    cot_z[0] = cot_blk[...]
    local[2].wait()
    wide[2 * FT : 3 * FT, :] = gt[...].T
    local[3].wait()
    wide[3 * FT : 4 * FT, :] = ut[...].T

    def assemble(k, group, blk, buf, whole):
        low = group * (E // 2)
        z_wait(k, lambda s: blk, buf, max(low, 1), low + E // 2)
        width = blk.shape[1]
        for i in range(E // 2):
            flat[i * R : (i + 1) * R, :width] = buf[low + i].astype(F32)
        mine = block(whole, c, y, group)
        mine[...] = flat[:, :width].astype(BF)
        for t in ys():
            go(y_copy(k, group, t, mine, mine, y))
        go(g_copy(k, group, y, mine))

    def pass_on(k, group, whole):
        for t in reversed(ys()):
            got = block(whole, c, t, group)
            y_copy(k, group, t, got, got, t).wait_recv()
            go(g_copy(k, group, t, got))

    def from_sibling(k, whole):
        for group in range(2):
            for t in range(NY):
                g_copy(k, group, t, block(whole, other, t, group)).wait_recv()

    def half_rows(core):
        return pl.ds(pl.multiple_of(core * HALF, HALF), HALF)

    def project(core):
        r = half_rows(core)
        v = nt(xt[r, :D], wide[...])
        speech = xt[r, D:].astype(F32) < 0.5
        p1[r, 0:FT] = jnp.where(speech, v[:, :FT], v[:, 2 * FT : 3 * FT])
        p1[r, FT : 2 * FT] = jnp.where(speech, v[:, FT : 2 * FT], v[:, 3 * FT : 4 * FT])
        p1[r, 2 * FT :] = v[:, 4 * FT :]

    def hidden_grad(core):
        r = half_rows(core)
        speech = xt[r, D:].astype(F32) < 0.5
        v = nt(ct[r, :], down[...])
        near = jnp.where(speech, v[:, :FT], v[:, FT : 2 * FT])
        tail = v[:, 2 * FT :]
        tail = jnp.concatenate([tail, jnp.zeros_like(tail)], axis=1)
        p2[r, 0:FT] = near
        p2[r, FT:] = tail
        p2b[r, 0:FT] = near.astype(BF)
        p2b[r, FT:] = tail.astype(BF)

    assemble(TOK, 0, tok_blk, tok_z, xt)
    assemble(TOK, 1, tok_blk, tok_z, xt)
    assemble(COT, 0, cot_blk, cot_z, ct)
    for copy in local[4:]:
        copy.wait()
    pass_on(TOK, 0, xt)
    assemble(COT, 1, cot_blk, cot_z, ct)
    pass_on(TOK, 1, xt)
    project(c)
    from_sibling(TOK, xt)
    project(other)
    for t in xs():
        go(x_copy(0, t, rows(p1, t), r1.at[x], x))
    pass_on(COT, 0, ct)
    pass_on(COT, 1, ct)
    hidden_grad(c)
    from_sibling(COT, ct)
    hidden_grad(other)
    for t in xs():
        go(x_copy(1, t, rows(p2b, t), r2.at[x], x))

    def split(v):
        return v[:, :FX], v[:, FX : 2 * FX]

    total = rows(p1, x)[...]
    for t in xs():
        x_copy(0, t, r1.at[t], r1.at[t], t).wait_recv()
        total += r1[t]
    gu[...] = total
    g, u = total[:, :FT], total[:, FT : 2 * FT]
    ge, ue = split(total[:, 2 * FT :])
    he = jax.nn.silu(ge) * ue
    mine = rows(hb, x)
    mine[:, 0:FT] = (jax.nn.silu(g) * u).astype(BF)
    mine[:, FT:] = jnp.concatenate([he, jnp.zeros_like(he)], axis=1).astype(BF)
    for t in xs():
        go(x_copy(2, t, mine, mine, x))

    total = rows(p2, x)[...]
    for t in xs():
        x_copy(1, t, r2.at[t], r2.at[t], t).wait_recv()
        total += r2[t].astype(F32)

    def back(dh, g, u):
        sig = jax.nn.sigmoid(g)
        return dh * u * sig * (1.0 + g * (1.0 - sig)), dh * (g * sig)

    dg, du = back(total[:, :FT], gu[:, :FT], gu[:, FT : 2 * FT])
    ge, ue = split(gu[:, 2 * FT :])
    dge, due = back(total[:, FT : FT + FX], ge, ue)
    mine_g = rows(gb, x)
    mine_g[:, 0:FT] = dg.astype(BF)
    mine_g[:, FT : 2 * FT] = du.astype(BF)
    mine_g[:, 2 * FT :] = jnp.concatenate([dge, due], axis=1).astype(BF)
    for t in xs():
        go(x_copy(3, t, mine_g, mine_g, x))

    def kinds(r):
        text = xt[r, D:]
        return (1.0 - text.astype(F32)).astype(BF), text

    def out_left(core):
        r = half_rows(core)
        speech, text = kinds(r)
        h = hb[r, 0:FT]
        hcat[r, 0:FT] = h * speech
        hcat[r, FT : 2 * FT] = h * text
        hcat[r, 2 * FT :] = hb[r, FT : FT + FX] * speech[:, :FX]
        return hcat[r, :]

    def grad_left(core):
        r = half_rows(core)
        speech, text = kinds(r)
        dg, du = gb[r, 0:FT], gb[r, FT : 2 * FT]
        return jnp.concatenate(
            [dg * speech, du * speech, dg * text, du * text, gb[r, 2 * FT :] * speech], axis=1
        )

    def partials(k, left, weights):
        rows_other = left(other)
        for n in range(D // NC):
            w = slice(n * NC, (n + 1) * NC)
            sib_src[k, :, w] = nn(rows_other, weights[:, w]).astype(BF)
            go(c_copy(k, n))
        rows_own = left(c)
        for n in range(D // NC):
            w = slice(n * NC, (n + 1) * NC)
            acc[k, :, w] = nn(rows_own, weights[:, w])

    def part(ref, k, t, group):
        return ref.at[k, pl.ds(pl.multiple_of(t * RB + group * RG, RG), RG)]

    def over_y(k):
        for n in range(D // NC):
            c_copy(k, n).wait_recv()
        for group in (1, 0):
            for t in ys():
                v = part(acc, k, t, group)[...] + part(sib_dst, k, t, group)[...].astype(F32)
                part(y_src, k, t, group)[...] = v.astype(BF)
                go(y_copy(2 + k, group, t, part(y_src, k, t, group), y_dst.at[k, group, y], y))

    def over_z(k):
        for group in (1, 0):
            total = part(acc, k, y, group)[...] + part(sib_dst, k, y, group)[...].astype(F32)
            for t in reversed(ys()):
                got = y_dst.at[k, group, t]
                y_copy(2 + k, group, t, got, got, t).wait_recv()
                total += got[...].astype(F32)
            low = group * (E // 2)
            for i in range(E // 2):
                z_src[k, low + i] = total[i * R : (i + 1) * R].astype(BF)
            z_send(2 + k, lambda s: z_src.at[k, s], z_dst.at[k], max(low, 1), low + E // 2)

    def finish(k, out):
        z_wait(2 + k, lambda s: z_src.at[k, s], z_dst.at[k], 1, E)
        total = z_src[k, 0].astype(F32)
        for i in range(1, E):
            total += z_dst[k, i].astype(F32)
        out[...] = total.astype(BF)

    def down_grads():
        left = hcat[...].T

        def body(n, _):
            w = pl.ds(pl.multiple_of(n * NC, NC), NC)
            v = nn(left, ct[:, w]).astype(BF)
            dsg[0:FT, w] = v[0:FT]
            dtg[:, w] = v[FT : 2 * FT]
            dsg[FT:, w] = v[2 * FT :]
            return 0

        lax.fori_loop(0, D // NC, body, 0)
        stores[0].start()
        stores[1].start()

    for t in xs():
        got = rows(hb, t)
        x_copy(2, t, got, got, t).wait_recv()
    partials(0, out_left, down)
    over_y(0)
    down_grads()
    for t in xs():
        got = rows(gb, t)
        x_copy(3, t, got, got, t).wait_recv()
    partials(1, grad_left, wide)
    over_y(1)
    over_z(0)
    over_z(1)
    finish(0, mixed)
    stores[2].start()
    finish(1, grad)
    stores[3].start()

    drain()
    for copy in stores:
        copy.wait()


def place(*refs):
    hold, sem = refs[8:12], refs[12]
    loads, stores = [], []
    for src, dst, mid in zip(refs[:4], refs[4:8], hold):
        strip = 64 if src.shape[0] % 64 == 0 else src.shape[0]
        for i in range(0, src.shape[0], strip):
            part, n = pl.ds(i, strip), len(loads)
            loads.append(pltpu.make_async_copy(src.at[part], mid.at[part], sem.at[0, n]))
            stores.append(pltpu.make_async_copy(mid.at[part], dst.at[part], sem.at[1, n]))
    for load in loads:
        load.start()
    for load, store in zip(loads, stores):
        load.wait()
        store.start()
    for store in stores:
        store.wait()


def shards(NY, E, S, tokens, modality, cotangent, *weights):
    R, D = tokens.shape
    gs, us, ds, gt, ut, dt = weights
    gs, us = gs.T, us.T
    FS, FT = gs.shape[0], gt.shape[1]
    RB = E * R
    HALF = NY * RB
    T = 2 * HALF
    CH = T // S
    DMA = pltpu.SemaphoreType.DMA
    hbm_spec = pl.BlockSpec(memory_space=pltpu.HBM)
    out_shape = (
        jax.ShapeDtypeStruct((R, D), BF),
        jax.ShapeDtypeStruct((R, D), BF),
        jax.ShapeDtypeStruct(ds.shape, BF),
        jax.ShapeDtypeStruct(dt.shape, BF),
    )
    outs = pl.pallas_call(
        functools.partial(kernel, NY, E, S),
        out_shape=out_shape,
        in_specs=[hbm_spec, pl.BlockSpec(memory_space=pltpu.SMEM)] + [hbm_spec] * 7,
        out_specs=[hbm_spec] * 4,
        scratch_shapes=[
            pltpu.VMEM(gt.shape, BF),
            pltpu.VMEM(ut.shape, BF),
            pltpu.VMEM((2 * (FS + FT), D), BF),
            pltpu.VMEM((FS + FT, D), BF),
            pltpu.VMEM((R, D + LANE), BF),
            pltpu.VMEM((R, D), BF),
            pltpu.VMEM((E, R, D + LANE), BF),
            pltpu.VMEM((E, R, D), BF),
            pltpu.VMEM((RB // 2, D + LANE), F32),
            pltpu.VMEM((T, D + LANE), BF),
            pltpu.VMEM((T, D), BF),
            pltpu.VMEM((T, 3 * FT), F32),
            pltpu.VMEM((T, 2 * FT), F32),
            pltpu.VMEM((T, 2 * FT), BF),
            pltpu.VMEM((S, CH, 3 * FT), F32),
            pltpu.VMEM((S, CH, 2 * FT), BF),
            pltpu.VMEM((CH, 3 * FT), F32),
            pltpu.VMEM((T, 2 * FT), BF),
            pltpu.VMEM((T, 3 * FT), BF),
            pltpu.VMEM((2, HALF, D), BF),
            pltpu.VMEM((2, HALF, D), BF),
            pltpu.VMEM((2, HALF, D), F32),
            pltpu.VMEM((2, HALF, D), BF),
            pltpu.VMEM((2, 2, NY, RB // 2, D), BF),
            pltpu.VMEM((2, E, R, D), BF),
            pltpu.VMEM((2, E, R, D), BF),
            pltpu.VMEM((T, FS + FT), BF),
            pltpu.VMEM((R, D), BF),
            pltpu.VMEM((R, D), BF),
            pltpu.VMEM(ds.shape, BF),
            pltpu.VMEM(dt.shape, BF),
            DMA((11,)),
            DMA((4,)),
            DMA((4, 2, E)),
            DMA((4, 2, 2, NY)),
            DMA((2, 2, 2, NY)),
            DMA((2, 2, 8)),
            DMA((4, 2, S)),
        ],
        compiler_params=pltpu.CompilerParams(
            collective_id=0, has_side_effects=True, vmem_limit_bytes=62 << 20
        ),
    )(tokens, modality, cotangent, gs, us, ds, gt, ut, dt)
    return pl.pallas_call(
        place,
        out_shape=out_shape,
        in_specs=[hbm_spec] * 4,
        out_specs=[hbm_spec] * 4,
        scratch_shapes=[pltpu.VMEM(o.shape, BF) for o in out_shape] + [DMA((2, 16))],
        compiler_params=pltpu.CompilerParams(vmem_limit_bytes=62 << 20),
    )(*outs)


def solution(mesh):
    NY, E, S = mesh.shape["attn"] // 2, mesh.shape["exp"], mesh.shape["seq"]
    row = P(("attn", "exp"), "seq")
    col = P("seq", ("attn", "exp"))
    return jax.shard_map(
        functools.partial(shards, NY, E, S),
        mesh=mesh,
        in_specs=(row, P(("attn", "exp")), row, col, col, row, col, col, row),
        out_specs=(row, row, row, row),
        check_vma=False,
    )
```

time: 81.6 us -> 70.8 us (0.87)
  Pallas kernels: 75.9 us -> 69.9 us
  local copies, waits for them, and re-layouts: 4.69 us -> 0 us
    pallas_call x1 -> x2, Pallas kernels: 75.9 us -> 69.9 us  [the longest x1 67.6 us: shards(): pl.pallas_call(functools.partial(kernel, NY, E, S), out_shape=out_shape,...]
    unnamed x10 -> x0, local copies, waits for them, and re-layouts: 4.69 us -> none
where the time goes in v2:
time: 70.8 us; the launch traced here: 70.5 us
  Pallas kernels  69.9 us (99%)
    pallas_call x1, Pallas kernels, shards(): pl.pallas_call(functools.partial(kernel, NY, E, S), out_shape=out_shape,...  67.6 us
    pallas_call x1, Pallas kernels, shards(): pl.pallas_call(place, out_shape=out_shape, in_specs=[hbm_spec] * 4, out_s...  2.27 us

profile of v2, /device:TPU:1, one launch (start us, length us, event | category | flops | bytes accessed | tf_op | source)
XLA Modules:
  0.0 70.5 jit_solution(14399860939592616213)
XLA Ops:
  0.6 67.6 %shard_map.120 = (bf16[2,1536]{1,0:T(2,128)(2,1)}, bf16[2,1536]{1,0:T(2,128)(2,1)}, bf16[192,1536]{1,0:T(8,128)(2,1)}, bf16[128,1536]{1,0:T(8,128)(2,1)}) custom-call(bf16[2,1536]{1,0:T(2,128)(2,1)} %tok.1, s32[2]{0:T(128)} %mod.1, bf16[2,1536]{1,0:T(2,128)(2,1)} %cot.1, bf16[192,1536]{1,0:T(8,128)(2,1)} %bitcast.2, bf16[192,1536]{1,0:T(8,128)(2,1)} %bitcast.3, ...), custom_call_target="tpu_custom_call" | custom-call | tf_op jit(solution)/shard_map/pallas_call | solution.py:425
  68.3 2.3 %shard_map.121 = (bf16[2,1536]{1,0:T(2,128)(2,1)}, bf16[2,1536]{1,0:T(2,128)(2,1)}, bf16[192,1536]{1,0:T(8,128)(2,1)}, bf16[128,1536]{1,0:T(8,128)(2,1)}) custom-call(bf16[2,1536]{1,0:T(2,128)(2,1)} %get-tuple-element.8.refs_0_, bf16[2,1536]{1,0:T(2,128)(2,1)} %get-tuple-element.9.refs_1_, bf16[192,1536]{1,0:T(8,128)(2,1)} %get-tuple-element.10.refs_2_, ...), custom_call_target="tpu_custom_call" | custom-call | tf_op jit(solution)/shard_map/pallas_call | solution.py:474

commit v3 on v2

--- a/solution.py
+++ b/solution.py
@@ -35,11 +35,11 @@
 def kernel(
     NY, E, S,
     tok, mod, cot, w_gs, w_us, w_ds, w_gt, w_ut, w_dt,
-    mixed_o, grad_o, dsg_o, dtg_o,
+    z_dst, dsg_o, dtg_o,
     gt, ut, wide, down,
     tok_blk, cot_blk, tok_z, cot_z, flat, xt, ct,
     p1, p2, p2b, r1, r2, gu, hb, gb,
-    sib_src, sib_dst, acc, y_src, y_dst, z_src, z_dst, hcat, mixed, grad, dsg, dtg,
+    sib_src, sib_dst, acc, y_src, y_dst, z_src, hcat, dsg, dtg,
     wsem, osem, zsem, ysem, gsem, csem, xsem,
 ):
     attn, z, x = lax.axis_index("attn"), lax.axis_index("exp"), lax.axis_index("seq")
@@ -53,6 +53,21 @@
     FS, FT = w_gs.shape[0], gt.shape[1]
     FX = FS - FT
     NC = 512 if D % 512 == 0 else D
+    W = E // 4
+
+    barrier = pltpu.get_barrier_semaphore()
+
+    def greet(device):
+        pl.semaphore_signal(barrier, inc=1, device_id=device, device_id_type=MESH)
+
+    for k in range(W, 0, -1):
+        greet({"exp": lax.rem(z + k, E)})
+        greet({"exp": lax.rem(z + E - k, E)})
+    for d in far_first(NY):
+        greet({"attn": lax.rem(y + d, NY) * 2 + c})
+    for d in far_first(S):
+        greet({"seq": lax.rem(x + d, S)})
+    greet({"attn": y * 2 + other})
 
     def load(src, at, size, dst, to, n):
         return pltpu.make_async_copy(src.at[pl.ds(at, size)], dst.at[pl.ds(to, size)], wsem.at[n])
@@ -75,25 +90,9 @@
     stores = [
         pltpu.make_async_copy(dsg, dsg_o, osem.at[0]),
         pltpu.make_async_copy(dtg, dtg_o, osem.at[1]),
-        pltpu.make_async_copy(mixed, mixed_o, osem.at[2]),
-        pltpu.make_async_copy(grad, grad_o, osem.at[3]),
+        pltpu.make_async_copy(z_src.at[0, 0], z_dst.at[0, 0], osem.at[2]),
+        pltpu.make_async_copy(z_src.at[1, 0], z_dst.at[1, 0], osem.at[3]),
     ]
-
-    def greet(axis, count, me, scale, base):
-        def body(d, _):
-            peer = lax.rem(me + d, count)
-            pl.semaphore_signal(
-                barrier, inc=1, device_id={axis: peer * scale + base}, device_id_type=MESH
-            )
-            return 0
-
-        lax.fori_loop(1, count, body, 0)
-
-    barrier = pltpu.get_barrier_semaphore()
-    greet("exp", E, z, 1, 0)
-    greet("attn", NY, y, 2, c)
-    greet("seq", S, x, 1, 0)
-    pl.semaphore_signal(barrier, inc=1, device_id={"attn": y * 2 + other}, device_id_type=MESH)
 
     local[0].wait()
     kind = jnp.concatenate(
@@ -101,7 +100,7 @@
     )
     tok_blk[:, D:] = kind.astype(BF)
     local[1].wait()
-    pl.semaphore_wait(barrier, (E - 1) + (NY - 1) + (S - 1) + 1)
+    pl.semaphore_wait(barrier, 2 * W + (NY - 1) + (S - 1) + 1)
 
     def ahead(s):
         return lax.rem(z + E + (s + 1) // 2 * (2 * (s % 2) - 1), E)
@@ -174,8 +173,25 @@
     def rows(ref, i):
         return ref.at[pl.ds(pl.multiple_of(i * CH, CH), CH)]
 
-    z_send(TOK, lambda s: tok_blk, tok_z, 1, E)
-    z_send(COT, lambda s: cot_blk, cot_z, 1, E)
+    def z_near(k, blk, buf):
+        z_send(k, lambda s: blk, buf, 1, 2 * W + 1)
+
+    def z_far(k, blk, buf):
+        z_wait(k, lambda s: blk, buf, 2 * W - 1, 2 * W + 1)
+        for j in range(W, 0, -1):
+            for at, to, peer in (
+                (2 * W, 2 * (W + j) if j < W else E - 1, z + j),
+                (2 * W - 1, 2 * (W + j) - 1, z + E - j),
+            )[: 2 if j < W else 1]:
+                go(
+                    remote(
+                        buf.at[at], buf.at[to], zsem.at[k, 0, to], zsem.at[k, 1, to],
+                        {"exp": lax.rem(peer, E)},
+                    )
+                )
+
+    z_near(TOK, tok_blk, tok_z)
+    z_near(COT, cot_blk, cot_z)
     tok_z[0] = tok_blk[...]
     cot_z[0] = cot_blk[...]
     local[2].wait()
@@ -185,7 +201,10 @@
 
     def assemble(k, group, blk, buf, whole):
         low = group * (E // 2)
-        z_wait(k, lambda s: blk, buf, max(low, 1), low + E // 2)
+        if group == 0:
+            z_wait(k, lambda s: blk, buf, 1, 2 * W - 1)
+        else:
+            z_wait(k, lambda s: blk, buf, 2 * W + 1, E)
         width = blk.shape[1]
         for i in range(E // 2):
             flat[i * R : (i + 1) * R, :width] = buf[low + i].astype(F32)
@@ -216,6 +235,13 @@
         p1[r, 0:FT] = jnp.where(speech, v[:, :FT], v[:, 2 * FT : 3 * FT])
         p1[r, FT : 2 * FT] = jnp.where(speech, v[:, FT : 2 * FT], v[:, 3 * FT : 4 * FT])
         p1[r, 2 * FT :] = v[:, 4 * FT :]
+
+    def x_half(k, core, src, dst):
+        for t in xs():
+
+            @pl.when(t // (S // 2) == core)
+            def _():
+                x_copy(k, t, rows(src, t), dst.at[x], x).start()
 
     def hidden_grad(core):
         r = half_rows(core)
@@ -229,7 +255,9 @@
         p2b[r, 0:FT] = near.astype(BF)
         p2b[r, FT:] = tail.astype(BF)
 
+    z_far(TOK, tok_blk, tok_z)
     assemble(TOK, 0, tok_blk, tok_z, xt)
+    z_far(COT, cot_blk, cot_z)
     assemble(TOK, 1, tok_blk, tok_z, xt)
     assemble(COT, 0, cot_blk, cot_z, ct)
     for copy in local[4:]:
@@ -238,17 +266,20 @@
     assemble(COT, 1, cot_blk, cot_z, ct)
     pass_on(TOK, 1, xt)
     project(c)
+    x_half(0, c, p1, r1)
     from_sibling(TOK, xt)
     project(other)
-    for t in xs():
-        go(x_copy(0, t, rows(p1, t), r1.at[x], x))
+    x_half(0, other, p1, r1)
     pass_on(COT, 0, ct)
     pass_on(COT, 1, ct)
     hidden_grad(c)
+    x_half(1, c, p2b, r2)
     from_sibling(COT, ct)
     hidden_grad(other)
-    for t in xs():
-        go(x_copy(1, t, rows(p2b, t), r2.at[x], x))
+    x_half(1, other, p2b, r2)
+    for t in xs():
+        pending.append(x_copy(0, t, rows(p1, t), r1.at[x], x).wait_send)
+        pending.append(x_copy(1, t, rows(p2b, t), r2.at[x], x).wait_send)
 
     def split(v):
         return v[:, :FX], v[:, FX : 2 * FX]
@@ -341,13 +372,7 @@
             for i in range(E // 2):
                 z_src[k, low + i] = total[i * R : (i + 1) * R].astype(BF)
             z_send(2 + k, lambda s: z_src.at[k, s], z_dst.at[k], max(low, 1), low + E // 2)
-
-    def finish(k, out):
-        z_wait(2 + k, lambda s: z_src.at[k, s], z_dst.at[k], 1, E)
-        total = z_src[k, 0].astype(F32)
-        for i in range(1, E):
-            total += z_dst[k, i].astype(F32)
-        out[...] = total.astype(BF)
+        stores[2 + k].start()
 
     def down_grads():
         left = hcat[...].T
@@ -377,30 +402,38 @@
     over_y(1)
     over_z(0)
     over_z(1)
-    finish(0, mixed)
-    stores[2].start()
-    finish(1, grad)
-    stores[3].start()
+    for k in range(2):
+        z_wait(2 + k, lambda s: z_src.at[k, s], z_dst.at[k], 1, E)
 
     drain()
     for copy in stores:
         copy.wait()
 
 
-def place(*refs):
-    hold, sem = refs[8:12], refs[12]
-    loads, stores = [], []
-    for src, dst, mid in zip(refs[:4], refs[4:8], hold):
+def place(slots, dsg, dtg, mixed_o, grad_o, dsg_o, dtg_o, slots_v, mixed, grad, dsg_v, dtg_v, sem):
+    def copies(src, dst, row):
         strip = 64 if src.shape[0] % 64 == 0 else src.shape[0]
-        for i in range(0, src.shape[0], strip):
-            part, n = pl.ds(i, strip), len(loads)
-            loads.append(pltpu.make_async_copy(src.at[part], mid.at[part], sem.at[0, n]))
-            stores.append(pltpu.make_async_copy(mid.at[part], dst.at[part], sem.at[1, n]))
-    for load in loads:
-        load.start()
+        return [
+            pltpu.make_async_copy(src.at[pl.ds(i, strip)], dst.at[pl.ds(i, strip)], sem.at[row, i // strip])
+            for i in range(0, src.shape[0], strip)
+        ]
+
+    parts = [pltpu.make_async_copy(slots.at[k], slots_v.at[k], sem.at[4, k]) for k in range(2)]
+    loads = copies(dsg, dsg_v, 0) + copies(dtg, dtg_v, 1)
+    stores = copies(dsg_v, dsg_o, 2) + copies(dtg_v, dtg_o, 3)
+    for copy in parts + loads:
+        copy.start()
     for load, store in zip(loads, stores):
         load.wait()
         store.start()
+    for k, (held, out) in enumerate(((mixed, mixed_o), (grad, grad_o))):
+        parts[k].wait()
+        total = slots_v[k, 0].astype(F32)
+        for i in range(1, slots_v.shape[1]):
+            total += slots_v[k, i].astype(F32)
+        held[...] = total.astype(BF)
+        stores.append(pltpu.make_async_copy(held, out, sem.at[5, k]))
+        stores[-1].start()
     for store in stores:
         store.wait()
 
@@ -416,17 +449,14 @@
     CH = T // S
     DMA = pltpu.SemaphoreType.DMA
     hbm_spec = pl.BlockSpec(memory_space=pltpu.HBM)
-    out_shape = (
-        jax.ShapeDtypeStruct((R, D), BF),
-        jax.ShapeDtypeStruct((R, D), BF),
-        jax.ShapeDtypeStruct(ds.shape, BF),
-        jax.ShapeDtypeStruct(dt.shape, BF),
-    )
+    slots = jax.ShapeDtypeStruct((2, E, R, D), BF)
+    own = jax.ShapeDtypeStruct((R, D), BF)
+    downs = (jax.ShapeDtypeStruct(ds.shape, BF), jax.ShapeDtypeStruct(dt.shape, BF))
     outs = pl.pallas_call(
         functools.partial(kernel, NY, E, S),
-        out_shape=out_shape,
+        out_shape=(slots, *downs),
         in_specs=[hbm_spec, pl.BlockSpec(memory_space=pltpu.SMEM)] + [hbm_spec] * 7,
-        out_specs=[hbm_spec] * 4,
+        out_specs=[hbm_spec] * 3,
         scratch_shapes=[
             pltpu.VMEM(gt.shape, BF),
             pltpu.VMEM(ut.shape, BF),
@@ -453,10 +483,7 @@
             pltpu.VMEM((2, HALF, D), BF),
             pltpu.VMEM((2, 2, NY, RB // 2, D), BF),
             pltpu.VMEM((2, E, R, D), BF),
-            pltpu.VMEM((2, E, R, D), BF),
             pltpu.VMEM((T, FS + FT), BF),
-            pltpu.VMEM((R, D), BF),
-            pltpu.VMEM((R, D), BF),
             pltpu.VMEM(ds.shape, BF),
             pltpu.VMEM(dt.shape, BF),
             DMA((11,)),
@@ -473,10 +500,10 @@
     )(tokens, modality, cotangent, gs, us, ds, gt, ut, dt)
     return pl.pallas_call(
         place,
-        out_shape=out_shape,
-        in_specs=[hbm_spec] * 4,
+        out_shape=(own, own, *downs),
+        in_specs=[hbm_spec] * 3,
         out_specs=[hbm_spec] * 4,
-        scratch_shapes=[pltpu.VMEM(o.shape, BF) for o in out_shape] + [DMA((2, 16))],
+        scratch_shapes=[pltpu.VMEM(o.shape, BF) for o in (slots, own, own, *downs)] + [DMA((6, 32))],
         compiler_params=pltpu.CompilerParams(vmem_limit_bytes=62 << 20),
     )(*outs)
 

time: 70.8 us -> 68 us (0.960)
  Pallas kernels: 69.9 us -> 66.6 us
    pallas_call x2, Pallas kernels: 69.9 us -> 66.6 us  [the longest x1 62.9 us: shards(): pl.pallas_call(functools.partial(kernel, NY, E, S), out_shape=(slots, *do...]
where the time goes in v3:
time: 68 us; the launch traced here: 67.3 us
  Pallas kernels  66.6 us (98%)
    pallas_call x1, Pallas kernels, shards(): pl.pallas_call(functools.partial(kernel, NY, E, S), out_shape=(slots, *do...  62.9 us
    pallas_call x1, Pallas kernels, shards(): pl.pallas_call(place, out_shape=(own, own, *downs), in_specs=[hbm_spec] *...  3.74 us

profile of v3, /device:TPU:1, one launch (start us, length us, event | category | flops | bytes accessed | tf_op | source)
XLA Modules:
  0.0 67.3 jit_solution(7391447623123146522)
XLA Ops:
  0.6 62.9 %shard_map.120 = (bf16[2,16,2,1536]{3,2,1,0:T(2,128)(2,1)}, bf16[192,1536]{1,0:T(8,128)(2,1)}, bf16[128,1536]{1,0:T(8,128)(2,1)}) custom-call(bf16[2,1536]{1,0:T(2,128)(2,1)} %tok.1, s32[2]{0:T(128)} %mod.1, bf16[2,1536]{1,0:T(2,128)(2,1)} %cot.1, bf16[192,1536]{1,0:T(8,128)(2,1)} %bitcast.2, bf16[192,1536]{1,0:T(8,128)(2,1)} %bitcast.3, ...), custom_call_target="tpu_custom_call" | custom-call | tf_op jit(solution)/shard_map/pallas_call | solution.py:455
  63.5 3.7 %shard_map.121 = (bf16[2,1536]{1,0:T(2,128)(2,1)}, bf16[2,1536]{1,0:T(2,128)(2,1)}, bf16[192,1536]{1,0:T(8,128)(2,1)}, bf16[128,1536]{1,0:T(8,128)(2,1)}) custom-call(bf16[2,16,2,1536]{3,2,1,0:T(2,128)(2,1)} %get-tuple-element.7.slots, bf16[192,1536]{1,0:T(8,128)(2,1)} %get-tuple-element.8.dsg, bf16[128,1536]{1,0:T(8,128)(2,1)} %get-tuple-element.9.dtg), custom_call_target="tpu_custom_call" | custom-call | tf_op jit(solution)/shard_map/pallas_call | solution.py:501

commit v4 on v2

--- a/solution.py
+++ b/solution.py
@@ -37,8 +37,8 @@
     tok, mod, cot, w_gs, w_us, w_ds, w_gt, w_ut, w_dt,
     mixed_o, grad_o, dsg_o, dtg_o,
     gt, ut, wide, down,
-    tok_blk, cot_blk, tok_z, cot_z, flat, xt, ct,
-    p1, p2, p2b, r1, r2, gu, hb, gb,
+    tok_blk, cot_blk, tok_z, cot_z, xt, ct,
+    p1, p2, r1, r2, gu, hb, gb,
     sib_src, sib_dst, acc, y_src, y_dst, z_src, z_dst, hcat, mixed, grad, dsg, dtg,
     wsem, osem, zsem, ysem, gsem, csem, xsem,
 ):
@@ -53,6 +53,21 @@
     FS, FT = w_gs.shape[0], gt.shape[1]
     FX = FS - FT
     NC = 512 if D % 512 == 0 else D
+    W = E // 4
+
+    barrier = pltpu.get_barrier_semaphore()
+
+    def greet(device):
+        pl.semaphore_signal(barrier, inc=1, device_id=device, device_id_type=MESH)
+
+    for k in range(W, 0, -1):
+        greet({"exp": lax.rem(z + k, E)})
+        greet({"exp": lax.rem(z + E - k, E)})
+    for d in far_first(NY):
+        greet({"attn": lax.rem(y + d, NY) * 2 + c})
+    for d in far_first(S):
+        greet({"seq": lax.rem(x + d, S)})
+    greet({"attn": y * 2 + other})
 
     def load(src, at, size, dst, to, n):
         return pltpu.make_async_copy(src.at[pl.ds(at, size)], dst.at[pl.ds(to, size)], wsem.at[n])
@@ -79,29 +94,13 @@
         pltpu.make_async_copy(grad, grad_o, osem.at[3]),
     ]
 
-    def greet(axis, count, me, scale, base):
-        def body(d, _):
-            peer = lax.rem(me + d, count)
-            pl.semaphore_signal(
-                barrier, inc=1, device_id={axis: peer * scale + base}, device_id_type=MESH
-            )
-            return 0
-
-        lax.fori_loop(1, count, body, 0)
-
-    barrier = pltpu.get_barrier_semaphore()
-    greet("exp", E, z, 1, 0)
-    greet("attn", NY, y, 2, c)
-    greet("seq", S, x, 1, 0)
-    pl.semaphore_signal(barrier, inc=1, device_id={"attn": y * 2 + other}, device_id_type=MESH)
-
     local[0].wait()
     kind = jnp.concatenate(
         [jnp.full((1, LANE), mod[i].astype(F32), F32) for i in range(R)], axis=0
     )
     tok_blk[:, D:] = kind.astype(BF)
     local[1].wait()
-    pl.semaphore_wait(barrier, (E - 1) + (NY - 1) + (S - 1) + 1)
+    pl.semaphore_wait(barrier, 2 * W + (NY - 1) + (S - 1) + 1)
 
     def ahead(s):
         return lax.rem(z + E + (s + 1) // 2 * (2 * (s % 2) - 1), E)
@@ -174,8 +173,25 @@
     def rows(ref, i):
         return ref.at[pl.ds(pl.multiple_of(i * CH, CH), CH)]
 
-    z_send(TOK, lambda s: tok_blk, tok_z, 1, E)
-    z_send(COT, lambda s: cot_blk, cot_z, 1, E)
+    def z_near(k, blk, buf):
+        z_send(k, lambda s: blk, buf, 1, 2 * W + 1)
+
+    def z_far(k, blk, buf):
+        z_wait(k, lambda s: blk, buf, 2 * W - 1, 2 * W + 1)
+        for j in range(W, 0, -1):
+            for at, to, peer in (
+                (2 * W, 2 * (W + j) if j < W else E - 1, z + j),
+                (2 * W - 1, 2 * (W + j) - 1, z + E - j),
+            )[: 2 if j < W else 1]:
+                go(
+                    remote(
+                        buf.at[at], buf.at[to], zsem.at[k, 0, to], zsem.at[k, 1, to],
+                        {"exp": lax.rem(peer, E)},
+                    )
+                )
+
+    z_near(TOK, tok_blk, tok_z)
+    z_near(COT, cot_blk, cot_z)
     tok_z[0] = tok_blk[...]
     cot_z[0] = cot_blk[...]
     local[2].wait()
@@ -185,12 +201,15 @@
 
     def assemble(k, group, blk, buf, whole):
         low = group * (E // 2)
-        z_wait(k, lambda s: blk, buf, max(low, 1), low + E // 2)
+        if group == 0:
+            z_wait(k, lambda s: blk, buf, 1, 2 * W - 1)
+        else:
+            z_wait(k, lambda s: blk, buf, 2 * W + 1, E)
         width = blk.shape[1]
-        for i in range(E // 2):
-            flat[i * R : (i + 1) * R, :width] = buf[low + i].astype(F32)
         mine = block(whole, c, y, group)
-        mine[...] = flat[:, :width].astype(BF)
+        mine[...] = jnp.concatenate(
+            [buf[low + i].astype(F32) for i in range(E // 2)], axis=0
+        ).astype(BF)
         for t in ys():
             go(y_copy(k, group, t, mine, mine, y))
         go(g_copy(k, group, y, mine))
@@ -216,6 +235,13 @@
         p1[r, 0:FT] = jnp.where(speech, v[:, :FT], v[:, 2 * FT : 3 * FT])
         p1[r, FT : 2 * FT] = jnp.where(speech, v[:, FT : 2 * FT], v[:, 3 * FT : 4 * FT])
         p1[r, 2 * FT :] = v[:, 4 * FT :]
+
+    def x_half(k, core, src, dst):
+        for t in xs():
+
+            @pl.when(t // (S // 2) == core)
+            def _():
+                x_copy(k, t, rows(src, t), dst.at[x], x).start()
 
     def hidden_grad(core):
         r = half_rows(core)
@@ -226,9 +252,9 @@
         tail = jnp.concatenate([tail, jnp.zeros_like(tail)], axis=1)
         p2[r, 0:FT] = near
         p2[r, FT:] = tail
-        p2b[r, 0:FT] = near.astype(BF)
-        p2b[r, FT:] = tail.astype(BF)
-
+
+    z_far(TOK, tok_blk, tok_z)
+    z_far(COT, cot_blk, cot_z)
     assemble(TOK, 0, tok_blk, tok_z, xt)
     assemble(TOK, 1, tok_blk, tok_z, xt)
     assemble(COT, 0, cot_blk, cot_z, ct)
@@ -238,17 +264,20 @@
     assemble(COT, 1, cot_blk, cot_z, ct)
     pass_on(TOK, 1, xt)
     project(c)
+    x_half(0, c, p1, r1)
     from_sibling(TOK, xt)
     project(other)
-    for t in xs():
-        go(x_copy(0, t, rows(p1, t), r1.at[x], x))
+    x_half(0, other, p1, r1)
     pass_on(COT, 0, ct)
     pass_on(COT, 1, ct)
     hidden_grad(c)
+    x_half(1, c, p2, r2)
     from_sibling(COT, ct)
     hidden_grad(other)
-    for t in xs():
-        go(x_copy(1, t, rows(p2b, t), r2.at[x], x))
+    x_half(1, other, p2, r2)
+    for t in xs():
+        pending.append(x_copy(0, t, rows(p1, t), r1.at[x], x).wait_send)
+        pending.append(x_copy(1, t, rows(p2, t), r2.at[x], x).wait_send)
 
     def split(v):
         return v[:, :FX], v[:, FX : 2 * FX]
@@ -270,7 +299,7 @@
     total = rows(p2, x)[...]
     for t in xs():
         x_copy(1, t, r2.at[t], r2.at[t], t).wait_recv()
-        total += r2[t].astype(F32)
+        total += r2[t]
 
     def back(dh, g, u):
         sig = jax.nn.sigmoid(g)
@@ -436,14 +465,12 @@
             pltpu.VMEM((R, D), BF),
             pltpu.VMEM((E, R, D + LANE), BF),
             pltpu.VMEM((E, R, D), BF),
-            pltpu.VMEM((RB // 2, D + LANE), F32),
             pltpu.VMEM((T, D + LANE), BF),
             pltpu.VMEM((T, D), BF),
             pltpu.VMEM((T, 3 * FT), F32),
             pltpu.VMEM((T, 2 * FT), F32),
-            pltpu.VMEM((T, 2 * FT), BF),
             pltpu.VMEM((S, CH, 3 * FT), F32),
-            pltpu.VMEM((S, CH, 2 * FT), BF),
+            pltpu.VMEM((S, CH, 2 * FT), F32),
             pltpu.VMEM((CH, 3 * FT), F32),
             pltpu.VMEM((T, 2 * FT), BF),
             pltpu.VMEM((T, 3 * FT), BF),

time: 70.8 us -> 66.6 us (0.941)
  Pallas kernels: 69.9 us -> 65.7 us
    pallas_call x1, Pallas kernels: 67.6 us -> 63.5 us  [shards(): pl.pallas_call(functools.partial(kernel, NY, E, S), out_shape=out_shape,...]
where the time goes in v4:
time: 66.6 us; the launch traced here: 66.4 us
  Pallas kernels  65.7 us (99%)
    pallas_call x1, Pallas kernels, shards(): pl.pallas_call(functools.partial(kernel, NY, E, S), out_shape=out_shape,...  63.5 us
    pallas_call x1, Pallas kernels, shards(): pl.pallas_call(place, out_shape=out_shape, in_specs=[hbm_spec] * 4, out_s...  2.27 us

profile of v4, /device:TPU:1, one launch (start us, length us, event | category | flops | bytes accessed | tf_op | source)
XLA Modules:
  0.0 66.4 jit_solution(17703604904170444877)
XLA Ops:
  0.6 63.5 %shard_map.120 = (bf16[2,1536]{1,0:T(2,128)(2,1)}, bf16[2,1536]{1,0:T(2,128)(2,1)}, bf16[192,1536]{1,0:T(8,128)(2,1)}, bf16[128,1536]{1,0:T(8,128)(2,1)}) custom-call(bf16[2,1536]{1,0:T(2,128)(2,1)} %tok.1, s32[2]{0:T(128)} %mod.1, bf16[2,1536]{1,0:T(2,128)(2,1)} %cot.1, bf16[192,1536]{1,0:T(8,128)(2,1)} %bitcast.2, bf16[192,1536]{1,0:T(8,128)(2,1)} %bitcast.3, ...), custom_call_target="tpu_custom_call" | custom-call | tf_op jit(solution)/shard_map/pallas_call | solution.py:454
  64.1 2.3 %shard_map.121 = (bf16[2,1536]{1,0:T(2,128)(2,1)}, bf16[2,1536]{1,0:T(2,128)(2,1)}, bf16[192,1536]{1,0:T(8,128)(2,1)}, bf16[128,1536]{1,0:T(8,128)(2,1)}) custom-call(bf16[2,1536]{1,0:T(2,128)(2,1)} %get-tuple-element.8.refs_0_, bf16[2,1536]{1,0:T(2,128)(2,1)} %get-tuple-element.9.refs_1_, bf16[192,1536]{1,0:T(8,128)(2,1)} %get-tuple-element.10.refs_2_, ...), custom_call_target="tpu_custom_call" | custom-call | tf_op jit(solution)/shard_map/pallas_call | solution.py:501

commit v5 on v4

--- a/solution.py
+++ b/solution.py
@@ -35,12 +35,12 @@
 def kernel(
     NY, E, S,
     tok, mod, cot, w_gs, w_us, w_ds, w_gt, w_ut, w_dt,
-    mixed_o, grad_o, dsg_o, dtg_o,
+    mixed, grad, dsg, dtg,
     gt, ut, wide, down,
     tok_blk, cot_blk, tok_z, cot_z, xt, ct,
     p1, p2, r1, r2, gu, hb, gb,
-    sib_src, sib_dst, acc, y_src, y_dst, z_src, z_dst, hcat, mixed, grad, dsg, dtg,
-    wsem, osem, zsem, ysem, gsem, csem, xsem,
+    sib_src, sib_dst, acc, y_src, y_dst, z_src, z_dst, hcat,
+    wsem, zsem, ysem, gsem, csem, xsem,
 ):
     attn, z, x = lax.axis_index("attn"), lax.axis_index("exp"), lax.axis_index("seq")
     y, c = attn // 2, attn % 2
@@ -87,12 +87,6 @@
     ]
     for copy in local:
         copy.start()
-    stores = [
-        pltpu.make_async_copy(dsg, dsg_o, osem.at[0]),
-        pltpu.make_async_copy(dtg, dtg_o, osem.at[1]),
-        pltpu.make_async_copy(mixed, mixed_o, osem.at[2]),
-        pltpu.make_async_copy(grad, grad_o, osem.at[3]),
-    ]
 
     local[0].wait()
     kind = jnp.concatenate(
@@ -110,9 +104,9 @@
 
     pending = []
 
-    def drain():
-        for wait in pending:
-            wait()
+    def drain(keep=0):
+        while len(pending) > keep:
+            pending.pop(0)()
 
     def go(copy):
         copy.start()
@@ -390,48 +384,43 @@
             return 0
 
         lax.fori_loop(0, D // NC, body, 0)
-        stores[0].start()
-        stores[1].start()
 
     for t in xs():
         got = rows(hb, t)
         x_copy(2, t, got, got, t).wait_recv()
     partials(0, out_left, down)
+    before = len(pending)
     over_y(0)
+    sent_y = len(pending) - before + D // NC
     down_grads()
     for t in xs():
         got = rows(gb, t)
         x_copy(3, t, got, got, t).wait_recv()
     partials(1, grad_left, wide)
+    before = len(pending)
     over_y(1)
+    drain(len(pending) - before + sent_y)
     over_z(0)
     over_z(1)
+    drain(2)
     finish(0, mixed)
-    stores[2].start()
+    drain()
     finish(1, grad)
-    stores[3].start()
 
     drain()
-    for copy in stores:
-        copy.wait()
 
 
 def place(*refs):
-    hold, sem = refs[8:12], refs[12]
-    loads, stores = [], []
-    for src, dst, mid in zip(refs[:4], refs[4:8], hold):
+    sem, copies = refs[8], []
+    for src, dst in zip(refs[:4], refs[4:8]):
         strip = 64 if src.shape[0] % 64 == 0 else src.shape[0]
         for i in range(0, src.shape[0], strip):
-            part, n = pl.ds(i, strip), len(loads)
-            loads.append(pltpu.make_async_copy(src.at[part], mid.at[part], sem.at[0, n]))
-            stores.append(pltpu.make_async_copy(mid.at[part], dst.at[part], sem.at[1, n]))
-    for load in loads:
-        load.start()
-    for load, store in zip(loads, stores):
-        load.wait()
-        store.start()
-    for store in stores:
-        store.wait()
+            part = pl.ds(i, strip)
+            copies.append(pltpu.make_async_copy(src.at[part], dst.at[part], sem.at[len(copies)]))
+    for copy in copies:
+        copy.start()
+    for copy in copies:
+        copy.wait()
 
 
 def shards(NY, E, S, tokens, modality, cotangent, *weights):
@@ -445,6 +434,7 @@
     CH = T // S
     DMA = pltpu.SemaphoreType.DMA
     hbm_spec = pl.BlockSpec(memory_space=pltpu.HBM)
+    vmem_spec = pl.BlockSpec(memory_space=pltpu.VMEM)
     out_shape = (
         jax.ShapeDtypeStruct((R, D), BF),
         jax.ShapeDtypeStruct((R, D), BF),
@@ -453,9 +443,9 @@
     )
     outs = pl.pallas_call(
         functools.partial(kernel, NY, E, S),
-        out_shape=out_shape,
+        out_shape=tuple(pltpu.VMEM(o.shape, BF) for o in out_shape),
         in_specs=[hbm_spec, pl.BlockSpec(memory_space=pltpu.SMEM)] + [hbm_spec] * 7,
-        out_specs=[hbm_spec] * 4,
+        out_specs=[vmem_spec] * 4,
         scratch_shapes=[
             pltpu.VMEM(gt.shape, BF),
             pltpu.VMEM(ut.shape, BF),
@@ -482,12 +472,7 @@
             pltpu.VMEM((2, E, R, D), BF),
             pltpu.VMEM((2, E, R, D), BF),
             pltpu.VMEM((T, FS + FT), BF),
-            pltpu.VMEM((R, D), BF),
-            pltpu.VMEM((R, D), BF),
-            pltpu.VMEM(ds.shape, BF),
-            pltpu.VMEM(dt.shape, BF),
             DMA((11,)),
-            DMA((4,)),
             DMA((4, 2, E)),
             DMA((4, 2, 2, NY)),
             DMA((2, 2, 2, NY)),
@@ -495,16 +480,16 @@
             DMA((4, 2, S)),
         ],
         compiler_params=pltpu.CompilerParams(
-            collective_id=0, has_side_effects=True, vmem_limit_bytes=62 << 20
+            collective_id=0, has_side_effects=True, vmem_limit_bytes=58 << 20
         ),
     )(tokens, modality, cotangent, gs, us, ds, gt, ut, dt)
     return pl.pallas_call(
         place,
         out_shape=out_shape,
-        in_specs=[hbm_spec] * 4,
+        in_specs=[vmem_spec] * 4,
         out_specs=[hbm_spec] * 4,
-        scratch_shapes=[pltpu.VMEM(o.shape, BF) for o in out_shape] + [DMA((2, 16))],
-        compiler_params=pltpu.CompilerParams(vmem_limit_bytes=62 << 20),
+        scratch_shapes=[DMA((16,))],
+        compiler_params=pltpu.CompilerParams(vmem_limit_bytes=16 << 20),
     )(*outs)
 
 

time: 66.6 us -> 64.7 us (0.971)
  Pallas kernels: 65.7 us -> 63.9 us
    pallas_call x2, Pallas kernels: 65.7 us -> 63.9 us  [the longest x1 62.8 us: shards(): pl.pallas_call(functools.partial(kernel, NY, E, S), out_shape=tuple((pltp...]
where the time goes in v5:
time: 64.7 us; the launch traced here: 64.5 us
  Pallas kernels  63.9 us (99%)
    pallas_call x1, Pallas kernels, shards(): pl.pallas_call(functools.partial(kernel, NY, E, S), out_shape=tuple((pltp...  62.8 us

profile of v5, /device:TPU:1, one launch (start us, length us, event | category | flops | bytes accessed | tf_op | source)
XLA Modules:
  0.0 64.5 jit_solution(6840019542913742686)
XLA Ops:
  0.6 62.8 %shard_map.120 = (bf16[2,1536]{1,0:T(2,128)(2,1)S(1)}, bf16[2,1536]{1,0:T(2,128)(2,1)S(1)}, bf16[192,1536]{1,0:T(8,128)(2,1)S(1)}, bf16[128,1536]{1,0:T(8,128)(2,1)S(1)}) custom-call(bf16[2,1536]{1,0:T(2,128)(2,1)} %tok.1, s32[2]{0:T(128)} %mod.1, bf16[2,1536]{1,0:T(2,128)(2,1)} %cot.1, bf16[192,1536]{1,0:T(8,128)(2,1)} %bitcast.2, ...), custom_call_target="tpu_custom_call" | custom-call | tf_op jit(solution)/shard_map/pallas_call | solution.py:444
  63.5 1.1 %shard_map.121 = (bf16[2,1536]{1,0:T(2,128)(2,1)}, bf16[2,1536]{1,0:T(2,128)(2,1)}, bf16[192,1536]{1,0:T(8,128)(2,1)}, bf16[128,1536]{1,0:T(8,128)(2,1)}) custom-call(bf16[2,1536]{1,0:T(2,128)(2,1)S(1)} %get-tuple-element.8.refs_0_, bf16[2,1536]{1,0:T(2,128)(2,1)S(1)} %get-tuple-element.9.refs_1_, bf16[192,1536]{1,0:T(8,128)(2,1)S(1)} %get-tuple-element.10.refs_2_, ...), custom_call_target="tpu_custom_call" | custom-call | tf_op jit(solution)/shard_map/pallas_call | solution.py:486

commit v6 on v5

--- a/solution.py
+++ b/solution.py
@@ -259,10 +259,10 @@
     pass_on(TOK, 1, xt)
     project(c)
     x_half(0, c, p1, r1)
+    pass_on(COT, 0, ct)
     from_sibling(TOK, xt)
     project(other)
     x_half(0, other, p1, r1)
-    pass_on(COT, 0, ct)
     pass_on(COT, 1, ct)
     hidden_grad(c)
     x_half(1, c, p2, r2)

time: 64.7 us -> 64.7 us (level)
  no operation moved by 1% of the time
where the time goes in v6:
time: 64.7 us; the launch traced here: 64.5 us
  Pallas kernels  63.9 us (99%)
    pallas_call x1, Pallas kernels, shards(): pl.pallas_call(functools.partial(kernel, NY, E, S), out_shape=tuple((pltp...  62.8 us

profile of v6, /device:TPU:1, one launch (start us, length us, event | category | flops | bytes accessed | tf_op | source)
XLA Modules:
  0.0 64.5 jit_solution(15804046926271441186)
XLA Ops:
  0.6 62.8 %shard_map.120 = (bf16[2,1536]{1,0:T(2,128)(2,1)S(1)}, bf16[2,1536]{1,0:T(2,128)(2,1)S(1)}, bf16[192,1536]{1,0:T(8,128)(2,1)S(1)}, bf16[128,1536]{1,0:T(8,128)(2,1)S(1)}) custom-call(bf16[2,1536]{1,0:T(2,128)(2,1)} %tok.1, s32[2]{0:T(128)} %mod.1, bf16[2,1536]{1,0:T(2,128)(2,1)} %cot.1, bf16[192,1536]{1,0:T(8,128)(2,1)} %bitcast.2, ...), custom_call_target="tpu_custom_call" | custom-call | tf_op jit(solution)/shard_map/pallas_call | solution.py:444
  63.5 1.1 %shard_map.121 = (bf16[2,1536]{1,0:T(2,128)(2,1)}, bf16[2,1536]{1,0:T(2,128)(2,1)}, bf16[192,1536]{1,0:T(8,128)(2,1)}, bf16[128,1536]{1,0:T(8,128)(2,1)}) custom-call(bf16[2,1536]{1,0:T(2,128)(2,1)S(1)} %get-tuple-element.8.refs_0_, bf16[2,1536]{1,0:T(2,128)(2,1)S(1)} %get-tuple-element.9.refs_1_, bf16[192,1536]{1,0:T(8,128)(2,1)S(1)} %get-tuple-element.10.refs_2_, ...), custom_call_target="tpu_custom_call" | custom-call | tf_op jit(solution)/shard_map/pallas_call | solution.py:486
